TPU v7x, 32 devices: a whole 2x2x4 slice. The times are simulated.
32 devices in a mesh: prow: 8 (over y, x, core), pcol: 4 (over z).
Axes of the slice: x: 2, y: 2, z: 4, core: 2. Of those that a mesh axis runs over, the one named last changes fastest.
Arguments:
- matrix: float32 [4096, 4096], P('prow', 'pcol'), may hold values from -6 to 6
- pivots: int32 [2, 512], replicated, may hold values from 0 to 4095, as said below
- lower_inv: float32 [2, 512, 512], replicated, as said below
- upper_inv: float32 [2, 512, 512], replicated, as said below
Outputs:
- factored: float32 [4096, 4096], P('prow', 'pcol')
Inputs may be any that keep to these rules, and one draw needn't show every extreme that they name: The entries of pivots[k] are distinct row indices from k * 512 to 4095. Each lower_inv[k] is lower triangular. Each upper_inv[k] is upper triangular.
All inputs are finite; a program needn't handle non-finite values.
Results may differ from a plain program's by a relative error of at most 0.0001.
Values sent between devices are 32-bit elements; how exact they have to be, the bound alone decides.
No kernel may reach another device: no remote copies, remote signals or barrier semaphores. Data moves between devices by JAX's collectives and lax.ppermute only.
A program may use at most 128 MiB of HBM per device.

v0:
```python
import jax
import jax.numpy as jnp
from jax import lax
from jax.sharding import PartitionSpec as P


def broadcast(block, axis, holder):
    block = jnp.where(lax.axis_index(axis) == holder, block, jnp.zeros_like(block))
    return lax.psum(block, axis)


def displaced(pivot_row, start_row):
    width = pivot_row.shape[0]
    end_row = start_row + width
    window = start_row + jnp.arange(width, dtype=jnp.int32)
    chosen = jnp.any(pivot_row[None, :] == window[:, None], axis=1)
    unnamed = jnp.logical_not(chosen)
    free_rank = jnp.cumsum(unnamed.astype(jnp.int32)) - 1
    outside = pivot_row >= end_row
    out_rank = jnp.sum(
        (outside[None, :] & (pivot_row[None, :] < pivot_row[:, None])).astype(jnp.int32), axis=1
    )
    matches = unnamed[None, :] & (free_rank[None, :] == out_rank[:, None])
    source = jnp.sum(jnp.where(matches, window[None, :], 0), axis=1)
    return (source, outside)


def product(left, right):
    return jnp.dot(left, right, precision=lax.Precision.HIGHEST, preferred_element_type=jnp.float32)


def shards(matrix, pivots, lower_inv, upper_inv):
    local_rows, local_cols = matrix.shape
    block_width = lower_inv.shape[1]
    first_row = lax.axis_index("prow") * local_rows
    row_ids = first_row + jnp.arange(local_rows, dtype=jnp.int32)
    col_ids = lax.axis_index("pcol") * local_cols + jnp.arange(local_cols, dtype=jnp.int32)
    current = matrix
    for panel_index in range(pivots.shape[0]):
        start_row = panel_index * block_width
        end_row = start_row + block_width
        wanted = pivots[panel_index]
        offset = wanted - first_row
        owned_rows = (offset >= 0) & (offset < local_rows)
        gathered_rows = jnp.take(current, jnp.clip(offset, 0, local_rows - 1), axis=0)
        picked = jnp.where(owned_rows[:, None], gathered_rows, 0.0)
        beyond = col_ids >= end_row
        reduced = lax.psum_scatter(picked, "prow", scatter_dimension=0, tiled=True)
        raw_top = lax.all_gather(reduced, "prow", axis=0, tiled=True)
        solved = product(lower_inv[panel_index], raw_top)
        top_block = jnp.where(beyond[None, :], solved, raw_top)
        top_masked = jnp.where(beyond[None, :], solved, 0.0)
        owner_row = start_row // local_rows
        first_local = start_row - owner_row * local_rows
        local_top = current
        old_top = broadcast(local_top, "prow", owner_row)
        source, outside = displaced(wanted, start_row)
        dest_local = jnp.where(outside & owned_rows, offset, local_rows)
        moved = jnp.take(old_top, jnp.clip(source - start_row, 0, block_width - 1), axis=0)
        swapped = current.at[dest_local].set(moved, mode="drop")
        is_owner = lax.axis_index("prow") == owner_row
        top_slice = swapped
        swapped = swapped.at[first_local : first_local + block_width].set(
            jnp.where(is_owner, top_block, top_slice)
        )
        owner_col = start_row // local_cols
        left_col = start_row - owner_col * local_cols
        column_panel = product(
            swapped[:, left_col : left_col + block_width], upper_inv[panel_index]
        )
        lower_block = broadcast(column_panel, "pcol", owner_col)
        below_rows = row_ids >= end_row
        lower_masked = jnp.where(below_rows[:, None], lower_block, 0.0)
        updated = swapped - product(lower_masked, top_masked)
        panel_slice = updated[:, left_col : left_col + block_width]
        col_owner = lax.axis_index("pcol") == owner_col
        new_panel = jnp.where(below_rows[:, None] & col_owner, lower_block, panel_slice)
        current = updated.at[:, left_col : left_col + block_width].set(new_panel)
    return current


def solution(mesh):
    in_specs = (P("prow", "pcol"), P(), P(), P())
    out_specs = P("prow", "pcol")
    return jax.shard_map(shards, mesh=mesh, in_specs=in_specs, out_specs=out_specs, check_vma=False)
```

profile of v0, /device:TPU:0, one launch (start us, length us, event | category | flops | bytes accessed | tf_op | source)
XLA Modules:
  0.0 474.5 jit_solution(15905027569336554562)
XLA Ops:
  10.8 2.9 copy.50
  13.8 3.2 select_select_fusion.1
  17.0 2.9 copy.72
  21.8 3.1 broadcast_select_fusion.1
  25.0 39.0 %reduce-scatter.7.cloned.1.call-done = f32[64,1024]{1,0:T(8,128)} async-done(((f32[512,1024]{1,0:T(8,128)}), f32[64,1024]{1,0:T(8,128)}) %reduce-scatter.7.cloned.1.call-update) | async-done | bytes 262160 | tf_op jit(solution)/shard_map/reduce_scatter | solution.py:48
  65.9 63.2 %all-reduce.5.cloned.1.call-done = f32[512,1024]{0,1:T(8,128)} async-done(((f32[512,1024]{0,1:T(8,128)}), f32[512,1024]{0,1:T(8,128)}) %all-reduce.5.cloned.1.call-update) | async-done | bytes 2097168 | tf_op jit(solution)/shard_map/psum | solution.py:9
  131.9 19.5 %scatter_custom_fusion = f32[512,1024]{1,0:T(8,128)S(1)} fusion(f32[512,1024]{1,0:T(8,128)S(1)} %copy.85, s32[512]{0:T(512)S(1)} %bitcast.75, f32[]{:T(128)} %constant.160.clone.4, pred[512]{0:T(512)(128)(4,1)S(1)} %compare_and_fusion.2, f32[512,1024]{1,0:T(8,128)} %copy.54, s32[1024]{0:T(1024)S(1)} %pad_clamp_fusion.2), kind=kCustom, calls=%fused_computation.17 | custom fusion | flops 524288 | bytes 4198916 | tf_op jit(solution)/shard_map/scatter | solution.py:60
  153.2 5.0 %all-gather.3.cloned.1.call-done = f32[512,1024]{1,0:T(8,128)} async-done(((f32[64,1024]{1,0:T(8,128)}), f32[512,1024]{1,0:T(8,128)}) %all-gather.3.cloned.1.call-update) | async-done | bytes 2097168 | tf_op jit(solution)/shard_map/all_gather | solution.py:49
  158.2 2.9 copy.52
  161.1 10.8 %fusion.2 = (f32[512,1024]{0,1:T(8,128)S(1)}, f32[1024,512]{1,0:T(8,128)}) fusion(f32[512,1024]{0,1:T(8,128)} %copy.55, f32[512,1024]{0,1:T(8,128)} %copy.52, pred[1024]{0:T(1024)(128)(4,1)S(1)} %fusion.41, pred[]{:T(512)S(6)} %eq.31, f32[512,1024]{1,0:T(8,128)} %all-gather.3.cloned.1.call-done, f32[2,512,512]{2,1,0:T(8,128)} %param.20), kind=kOutput, calls=%fused_computation.12 | convolution fusion | flops 3222274048 | bytes 11535361 | tf_op jit(solution)/shard_map/dot_general | solution.py:29
  171.9 2.9 convolution_select_fusion.1
  175.7 51.7 %all-reduce.7.cloned.1.call-done = f32[512,512]{0,1:T(8,128)} async-done(((f32[512,512]{0,1:T(8,128)}), f32[512,512]{0,1:T(8,128)}) %all-reduce.7.cloned.1.call-update) | async-done | bytes 1048592 | tf_op jit(solution)/shard_map/psum | solution.py:9
  227.4 6.9 %fusion.8 = f32[512,1024]{0,1:T(8,128)} fusion(f32[512,1024]{0,1:T(8,128)S(1)} %get-tuple-element.86, f32[1024,512]{1,0:T(8,128)} %get-tuple-element.87, f32[512,512]{0,1:T(8,128)} %all-reduce.7.cloned.1.call-done, pred[1024]{0:T(1024)(128)(4,1)S(1)} %fusion.41, pred[512]{0:T(512)(128)(4,1)S(1)} %fusion.44), kind=kOutput, calls=%fused_computation.20 | convolution fusion | flops 3222536192 | bytes 7341568 | tf_op jit(solution)/shard_map/dot_general | solution.py:29
  234.3 3.0 fusion.10
  244.8 3.2 select_select_fusion
  252.6 39.1 %reduce-scatter.9.cloned.1.call-done = f32[64,1024]{1,0:T(8,128)} async-done(((f32[512,1024]{1,0:T(8,128)}), f32[64,1024]{1,0:T(8,128)}) %reduce-scatter.9.cloned.1.call-update) | async-done | bytes 262160 | tf_op jit(solution)/shard_map/reduce_scatter | solution.py:48
  293.0 63.5 %all-reduce.9.cloned.1.call-done = f32[512,1024]{0,1:T(8,128)} async-done(((f32[512,1024]{0,1:T(8,128)}), f32[512,1024]{0,1:T(8,128)}) %all-reduce.9.cloned.1.call-update) | async-done | bytes 2097168 | tf_op jit(solution)/shard_map/psum | solution.py:9
  359.4 19.6 %scatter_custom_fusion.1 = f32[512,1024]{1,0:T(8,128)S(1)} fusion(f32[512,1024]{1,0:T(8,128)S(1)} %copy.58, s32[512]{0:T(512)S(1)} %bitcast.74, f32[]{:T(128)} %constant.160.clone.4, pred[512]{0:T(512)(128)(4,1)S(1)} %compare_and_fusion, f32[512,1024]{1,0:T(8,128)} %copy.62, s32[1024]{0:T(1024)S(1)} %pad_clamp_fusion), kind=kCustom, calls=%fused_computation.14 | custom fusion | flops 524288 | bytes 4198916 | tf_op jit(solution)/shard_map/scatter | solution.py:60
  380.8 4.9 %all-gather.5.cloned.1.call-done = f32[512,1024]{1,0:T(8,128)} async-done(((f32[64,1024]{1,0:T(8,128)}), f32[512,1024]{1,0:T(8,128)}) %all-gather.5.cloned.1.call-update) | async-done | bytes 2097168 | tf_op jit(solution)/shard_map/all_gather | solution.py:49
  385.7 3.1 copy.61
  388.8 11.4 %fusion = (f32[512,1024]{0,1:T(8,128)S(1)}, f32[1024,512]{1,0:T(8,128)}) fusion(f32[512,1024]{0,1:T(8,128)} %copy.64, f32[512,1024]{0,1:T(8,128)} %copy.61, pred[1024]{0:T(1024)(128)(4,1)S(1)} %fusion.42, pred[]{:T(512)S(6)} %eq.30, f32[512,1024]{1,0:T(8,128)} %all-gather.5.cloned.1.call-done, f32[2,512,512]{2,1,0:T(8,128)} %param.20), kind=kOutput, calls=%fused_computation.8 | convolution fusion | flops 3222274048 | bytes 11535361 | tf_op jit(solution)/shard_map/dot_general | solution.py:29
  400.3 2.9 convolution_select_fusion
  403.2 51.9 %all-reduce.11.cloned.1.call-done = f32[512,512]{0,1:T(8,128)} async-done(((f32[512,512]{0,1:T(8,128)}), f32[512,512]{0,1:T(8,128)}) %all-reduce.11.cloned.1.call-update) | async-done | bytes 1048592 | tf_op jit(solution)/shard_map/psum | solution.py:9
  455.2 6.9 %fusion.9 = f32[512,1024]{0,1:T(8,128)} fusion(f32[512,1024]{0,1:T(8,128)S(1)} %get-tuple-element.88, f32[1024,512]{1,0:T(8,128)} %get-tuple-element.89, f32[512,512]{0,1:T(8,128)} %all-reduce.11.cloned.1.call-done, pred[1024]{0:T(1024)(128)(4,1)S(1)} %fusion.42, pred[512]{0:T(512)(128)(4,1)S(1)} %fusion.43), kind=kOutput, calls=%fused_computation.21 | convolution fusion | flops 3222536192 | bytes 7341568 | tf_op jit(solution)/shard_map/dot_general | solution.py:29
  (78 shorter events, 37.1 us)
Async XLA Ops:
  6.5 1.6 copy-start.4
  6.5 57.4 %reduce-scatter.7.cloned.1.call-start = ((), (), s32[]{:S(2)}) async-start(), calls=%async_computation.8 | async-start | bytes 2359296 | tf_op jit(solution)/shard_map/reduce_scatter | solution.py:48
  19.9 109.1 %all-reduce.5.cloned.1.call-start = ((), (), s32[]{:S(2)}) async-start(), calls=%async_computation.3 | async-start | bytes 4194304 | tf_op jit(solution)/shard_map/psum | solution.py:9
  25.0 133.2 %all-gather.3.cloned.1.call-start = ((), (), s32[]{:S(2)}) async-start(), calls=%async_computation.2 | async-start | bytes 2359296 | tf_op jit(solution)/shard_map/all_gather | solution.py:49
  64.0 163.4 %all-reduce.7.cloned.1.call-start = ((), (), s32[]{:S(2)}) async-start(), calls=%async_computation.4 | async-start | bytes 2097152 | tf_op jit(solution)/shard_map/psum | solution.py:9
  161.1 10.8 %copy-start.2 = (f32[2,512,512]{2,1,0:T(8,128)S(1)}, f32[2,512,512]{2,1,0:T(8,128)}, u32[]{:S(2)}) copy-start(f32[2,512,512]{2,1,0:T(8,128)} %param.21) | copy-start | bytes 6291460
  174.8 116.8 %reduce-scatter.9.cloned.1.call-start = ((), (), s32[]{:S(2)}) async-start(), calls=%async_computation.9 | async-start | bytes 2359296 | tf_op jit(solution)/shard_map/reduce_scatter | solution.py:48
  227.4 6.9 %copy-start = (f32[512,512]{0,1:T(8,128)S(1)}, f32[512,512]{0,1:T(8,128)}, u32[]{:S(2)}) copy-start(f32[512,512]{0,1:T(8,128)} %all-reduce.7.cloned.1.call-done) | copy-start | bytes 3145732
  250.9 105.7 %all-reduce.9.cloned.1.call-start = ((), (), s32[]{:S(2)}) async-start(), calls=%async_computation.6 | async-start | bytes 4194304 | tf_op jit(solution)/shard_map/psum | solution.py:9
  252.5 133.2 %all-gather.5.cloned.1.call-start = ((), (), s32[]{:S(2)}) async-start(), calls=%async_computation.5 | async-start | bytes 2359296 | tf_op jit(solution)/shard_map/all_gather | solution.py:49
  291.7 163.5 %all-reduce.11.cloned.1.call-start = ((), (), s32[]{:S(2)}) async-start(), calls=%async_computation.7 | async-start | bytes 2097152 | tf_op jit(solution)/shard_map/psum | solution.py:9
  388.8 11.4 %copy-start.3 = (f32[2,512,512]{2,1,0:T(8,128)S(1)}, f32[2,512,512]{2,1,0:T(8,128)}, u32[]{:S(2)}) copy-start(f32[2,512,512]{2,1,0:T(8,128)} %param.21) | copy-start | bytes 6291460
  455.2 6.9 %copy-start.1 = (f32[512,512]{0,1:T(8,128)S(1)}, f32[512,512]{0,1:T(8,128)}, u32[]{:S(2)}) copy-start(f32[512,512]{0,1:T(8,128)} %all-reduce.11.cloned.1.call-done) | copy-start | bytes 3145732
Sparse Core Ops, SparseCore 0:
  20.0 43.8 reduce-scatter.6
  67.5 61.4 all-reduce.4
  131.1 27.0 all-gather.2
  175.0 52.4 all-reduce.6
  251.0 40.5 reduce-scatter.8
  295.1 61.4 all-reduce.8
  358.6 27.0 all-gather.4
  403.3 51.8 all-reduce.10
where the time goes:
time: 482 us; the launch traced here: 474 us
  waiting for transfers between devices  318 us (66%)
  other arithmetic  59 us (12%)
  matrix products  41.9 us (9%)
  local copies, waits for them, and re-layouts  41 us (9%)
  between operations  13.9 us (3%)
    psum x4, waiting for transfers between devices, broadcast(): return lax.psum(block, axis)  230 us
    reduce_scatter x2, waiting for transfers between devices, shards(): reduced = lax.psum_scatter(picked, 'prow', scatter_dimension=0, tiled=True)  78 us
    dot_general x6, matrix products, product(): jnp.dot(left, right, precision=lax.Precision.HIGHEST, preferred_element_t...  41.9 us
    scatter x2, other arithmetic, shards(): swapped = current.at[dest_local].set(moved, mode='drop')  39.1 us
    gather x4, local copies, waits for them, and re-layouts, shards(): jnp.take(current, jnp.clip(offset, 0, local_rows - 1), axis=0)  11.1 us
    all_gather x2, waiting for transfers between devices, shards(): raw_top = lax.all_gather(reduced, 'prow', axis=0, tiled=True)  9.83 us
  transfers between devices with their start and end apart: 8, of which 8 were waited for; matrix products, arithmetic and copies ran while one was open for 12% of the time, Pallas kernels for 0%

commit v1 on v0

--- a/solution.py
+++ b/solution.py
@@ -2,6 +2,28 @@
 import jax.numpy as jnp
 from jax import lax
 from jax.sharding import PartitionSpec as P
+
+
+def joined_along(blocks, dim):
+    shape = list(blocks.shape[1:])
+    shape[dim] *= blocks.shape[0]
+    return jnp.moveaxis(blocks, 0, dim).reshape(shape)
+
+
+def collected_by_bits(value, axis):
+    count = lax.axis_size(axis)
+    blocks = value[None]
+    for level in range(count.bit_length() - 1):
+        stride = 1 << level
+        received = lax.ppermute(blocks, axis, [(i, i ^ stride) for i in range(count)])
+        both = jnp.stack([blocks, received])
+        upper = lax.axis_index(axis) >> level & 1
+        blocks = jnp.where(upper == 0, both, both[::-1]).reshape(-1, *value.shape)
+    return blocks
+
+
+def collect(shard, axis, dim):
+    return joined_along(collected_by_bits(shard, axis), dim)
 
 
 def broadcast(block, axis, holder):
@@ -46,7 +68,7 @@
         picked = jnp.where(owned_rows[:, None], gathered_rows, 0.0)
         beyond = col_ids >= end_row
         reduced = lax.psum_scatter(picked, "prow", scatter_dimension=0, tiled=True)
-        raw_top = lax.all_gather(reduced, "prow", axis=0, tiled=True)
+        raw_top = collect(reduced, "prow", 0)
         solved = product(lower_inv[panel_index], raw_top)
         top_block = jnp.where(beyond[None, :], solved, raw_top)
         top_masked = jnp.where(beyond[None, :], solved, 0.0)

time: 482 us -> 498 us (1.033)
  local copies, waits for them, and re-layouts: 41 us -> 58.9 us
  waiting for transfers between devices: 318 us -> 303 us
  other arithmetic: 59 us -> 71.1 us
  matrix products: 41.9 us -> 36.6 us
    unnamed x8, waiting for transfers between devices: 0.13 us -> 83 us
    reduce_scatter x2 -> x0, waiting for transfers between devices: 78 us -> none  [shards(): reduced = lax.psum_scatter(picked, 'prow', scatter_dimension=0, tiled=True)]
    psum x4, waiting for transfers between devices: 230 us -> 183 us  [broadcast(): return lax.psum(block, axis)]
    ppermute x0 -> x6, waiting for transfers between devices: none -> 37.8 us  [collected_by_bits(): lax.ppermute(blocks, axis, [(i, i ^ stride) for i in range(count)])]
    all_gather x2 -> x0, waiting for transfers between devices: 9.83 us -> none  [shards(): raw_top = lax.all_gather(reduced, 'prow', axis=0, tiled=True)]
    unnamed x14 -> x36, local copies, waits for them, and re-layouts: 9.27 us -> 17.9 us
    another operation x5 -> x13, other arithmetic: 1.29 us -> 9.25 us  [the longest x8 7.92 us: collected_by_bits(): both = jnp.stack([blocks, received])]
    all_gather x2 -> x0, local copies, waits for them, and re-layouts: 5.97 us -> none  [shards(): raw_top = lax.all_gather(reduced, 'prow', axis=0, tiled=True)]
  transfers between devices with their start and end apart: 8 -> 12, of which waited for: 8 -> 9; matrix products, arithmetic and copies ran while one was open for 12% -> 16% of each run, Pallas kernels for 0% -> 0%
where the time goes in v1:
time: 498 us; the launch traced here: 489 us
  waiting for transfers between devices  303 us (61%)
  other arithmetic  71.1 us (14%)
  local copies, waits for them, and re-layouts  58.9 us (12%)
  matrix products  36.6 us (7%)
  between operations  14.1 us (3%)
    psum x4, waiting for transfers between devices, broadcast(): return lax.psum(block, axis)  183 us
    unnamed x8, waiting for transfers between devices  83 us
    scatter x2, other arithmetic, shards(): swapped = current.at[dest_local].set(moved, mode='drop')  39.2 us
    ppermute x6, waiting for transfers between devices, collected_by_bits(): lax.ppermute(blocks, axis, [(i, i ^ stride) for i in range(count)])  37.8 us
    dot_general x6, matrix products, product(): jnp.dot(left, right, precision=lax.Precision.HIGHEST, preferred_element_t...  36.6 us
    unnamed x36, local copies, waits for them, and re-layouts  17.9 us
    gather x4, local copies, waits for them, and re-layouts, shards(): jnp.take(current, jnp.clip(offset, 0, local_rows - 1), axis=0)  11.2 us
  transfers between devices with their start and end apart: 12, of which 9 were waited for; matrix products, arithmetic and copies ran while one was open for 16% of the time, Pallas kernels for 0%

profile of v1, /device:TPU:0, one launch (start us, length us, event | category | flops | bytes accessed | tf_op | source)
XLA Modules:
  0.0 489.0 jit_solution(2268442098345026334)
XLA Ops:
  10.8 2.9 copy.71
  13.8 3.2 select_select_fusion.1
  17.0 2.9 copy.100
  21.8 42.2 %reduce-scatter.7.cloned.1.call-done = f32[64,1024]{1,0:T(8,128)} async-done(((f32[512,1024]{1,0:T(8,128)}), f32[64,1024]{1,0:T(8,128)}) %reduce-scatter.7.cloned.1.call-update) | async-done | bytes 262160
  65.2 3.1 broadcast_select_fusion.1
  71.6 20.8 %collective-permute-done.1 = f32[2,64,1024]{2,1,0:T(8,128)} collective-permute-done((f32[2,64,1024]{2,1,0:T(8,128)}, f32[2,64,1024]{2,1,0:T(8,128)}, u32[]{:S(2)}, u32[]{:S(2)}) %collective-permute-start.1) | collective-permute-done | bytes 524320 | tf_op jit(solution)/shard_map/ppermute | solution.py:18
  102.4 37.1 %all-reduce.5.cloned.1.call-done = f32[512,1024]{0,1:T(8,128)} async-done(((f32[512,1024]{0,1:T(8,128)}), f32[512,1024]{0,1:T(8,128)}) %all-reduce.5.cloned.1.call-update) | async-done | bytes 2097168 | tf_op jit(solution)/shard_map/psum | solution.py:31
  139.6 2.9 copy.79
  142.4 19.4 %scatter_custom_fusion = f32[512,1024]{1,0:T(8,128)S(1)} fusion(f32[512,1024]{1,0:T(8,128)S(1)} %copy.113, s32[512]{0:T(512)S(1)} %bitcast.117, f32[]{:T(128)} %constant.161.clone.4, pred[512]{0:T(512)(128)(4,1)S(1)} %compare_and_fusion.2, f32[512,1024]{1,0:T(8,128)} %copy.79, s32[1024]{0:T(1024)S(1)} %pad_clamp_fusion.2), kind=kCustom, calls=%fused_computation.25 | custom fusion | flops 524288 | bytes 4198916 | tf_op jit(solution)/shard_map/scatter | solution.py:82
  168.5 8.7 %fusion.18 = f32[1024,512]{1,0:T(8,128)S(1)} fusion(f32[512,1024]{1,0:T(8,128)} %bitcast.97, f32[2,512,512]{2,1,0:T(8,128)} %param.20), kind=kOutput, calls=%fused_computation.46 | convolution fusion | flops 3221225472 | bytes 5242880 | tf_op jit(solution)/shard_map/dot_general | solution.py:51
  179.4 2.9 convolution_select_fusion.1
  183.3 50.3 %all-reduce.7.cloned.1.call-done = f32[512,512]{0,1:T(8,128)} async-done(((f32[512,512]{0,1:T(8,128)}), f32[512,512]{0,1:T(8,128)}) %all-reduce.7.cloned.1.call-update) | async-done | bytes 1048592 | tf_op jit(solution)/shard_map/psum | solution.py:31
  233.6 6.7 %fusion.8 = f32[512,1024]{0,1:T(8,128)} fusion(f32[512,1024]{0,1:T(8,128)} %copy-done.2, f32[1024,512]{1,0:T(8,128)S(1)} %fusion.18, f32[512,512]{0,1:T(8,128)} %all-reduce.7.cloned.1.call-done, pred[1024]{0:T(1024)(128)(4,1)S(1)} %fusion.45, pred[512]{0:T(512)(128)(4,1)S(1)} %get-tuple-element.90), kind=kOutput, calls=%fused_computation.28 | convolution fusion | flops 3222536192 | bytes 7341568 | tf_op jit(solution)/shard_map/dot_general | solution.py:51
  240.3 3.0 fusion.10
  247.9 2.9 copy.84
  250.8 3.2 select_select_fusion
  254.0 2.9 copy.102
  257.0 40.7 %reduce-scatter.9.cloned.1.call-done = f32[64,1024]{1,0:T(8,128)} async-done(((f32[512,1024]{1,0:T(8,128)}), f32[64,1024]{1,0:T(8,128)}) %reduce-scatter.9.cloned.1.call-update) | async-done | bytes 262160
  306.2 15.4 %collective-permute-done.4 = f32[2,64,1024]{2,1,0:T(8,128)} collective-permute-done((f32[2,64,1024]{2,1,0:T(8,128)}, f32[2,64,1024]{2,1,0:T(8,128)}, u32[]{:S(2)}, u32[]{:S(2)}) %collective-permute-start.4) | collective-permute-done | bytes 524320 | tf_op jit(solution)/shard_map/ppermute | solution.py:18
  331.4 44.1 %all-reduce.9.cloned.1.call-done = f32[512,1024]{0,1:T(8,128)} async-done(((f32[512,1024]{0,1:T(8,128)}), f32[512,1024]{0,1:T(8,128)}) %all-reduce.9.cloned.1.call-update) | async-done | bytes 2097168 | tf_op jit(solution)/shard_map/psum | solution.py:31
  378.4 19.8 %scatter_custom_fusion.1 = f32[512,1024]{1,0:T(8,128)S(1)} fusion(f32[512,1024]{1,0:T(8,128)S(1)} %copy.83, s32[512]{0:T(512)S(1)} %bitcast.116, f32[]{:T(128)} %constant.161.clone.4, pred[512]{0:T(512)(128)(4,1)S(1)} %compare_and_fusion, f32[512,1024]{1,0:T(8,128)} %copy.90, s32[1024]{0:T(1024)S(1)} %pad_clamp_fusion), kind=kCustom, calls=%fused_computation.22 | custom fusion | flops 524288 | bytes 4198916 | tf_op jit(solution)/shard_map/scatter | solution.py:82
  404.8 8.7 %fusion.15 = f32[1024,512]{1,0:T(8,128)S(1)} fusion(f32[512,1024]{1,0:T(8,128)} %bitcast.95, f32[2,512,512]{2,1,0:T(8,128)} %param.20), kind=kOutput, calls=%fused_computation.43 | convolution fusion | flops 3221225472 | bytes 5242880 | tf_op jit(solution)/shard_map/dot_general | solution.py:51
  418.7 51.1 %all-reduce.11.cloned.1.call-done = f32[512,512]{0,1:T(8,128)} async-done(((f32[512,512]{0,1:T(8,128)}), f32[512,512]{0,1:T(8,128)}) %all-reduce.11.cloned.1.call-update) | async-done | bytes 1048592 | tf_op jit(solution)/shard_map/psum | solution.py:31
  469.8 6.7 %fusion.9 = f32[512,1024]{0,1:T(8,128)} fusion(f32[512,1024]{0,1:T(8,128)} %copy-done.3, f32[1024,512]{1,0:T(8,128)S(1)} %fusion.15, f32[512,512]{0,1:T(8,128)} %all-reduce.11.cloned.1.call-done, pred[1024]{0:T(1024)(128)(4,1)S(1)} %fusion.46, pred[512]{0:T(512)(128)(4,1)S(1)} %fusion.47), kind=kOutput, calls=%fused_computation.29 | convolution fusion | flops 3222536192 | bytes 7341568 | tf_op jit(solution)/shard_map/dot_general | solution.py:51
  (125 shorter events, 73.2 us)
Async XLA Ops:
  6.5 1.6 copy-start.14
  6.5 57.4 %reduce-scatter.7.cloned.1.call-start = ((), (), s32[]{:S(2)}) async-start(), calls=%async_computation.6 | async-start | bytes 2359296
  19.9 119.6 %all-reduce.5.cloned.1.call-start = ((), (), s32[]{:S(2)}) async-start(), calls=%async_computation.2 | async-start | bytes 4194304 | tf_op jit(solution)/shard_map/psum | solution.py:31
  65.1 3.5 collective-permute-start
  68.4 165.2 %all-reduce.7.cloned.1.call-start = ((), (), s32[]{:S(2)}) async-start(), calls=%async_computation.3 | async-start | bytes 2097152 | tf_op jit(solution)/shard_map/psum | solution.py:31
  70.9 23.8 %copy-start.8 = (f32[1,2,64,1024]{2,3,1,0:T(8,128)S(1)}, f32[1,2,64,1024]{2,3,1,0:T(8,128)}, u32[]{:S(2)}) copy-start(f32[1,2,64,1024]{2,3,1,0:T(8,128)} %get-tuple-element.78) | copy-start | bytes 1572868
  70.9 21.5 %collective-permute-start.1 = (f32[2,64,1024]{2,1,0:T(8,128)}, f32[2,64,1024]{2,1,0:T(8,128)}, u32[]{:S(2)}, u32[]{:S(2)}) collective-permute-start(f32[2,64,1024]{2,1,0:T(8,128)} %copy.73), channel_id=1, source_target_pairs={{0,8},{4,12},{8,0},{12,4},{16,24},{20,28},{24,16},{28,20},{1,9},{5... | collective-permute-start | bytes 1572872 | tf_op jit(solution)/shard_map/ppermute | solution.py:18
  99.9 63.8 %collective-permute-start.2 = (f32[4,64,1024]{2,1,0:T(8,128)S(1)}, f32[4,64,1024]{2,1,0:T(8,128)}, u32[]{:S(2)}, u32[]{:S(2)}) collective-permute-start(f32[4,64,1024]{2,1,0:T(8,128)S(1)} %bitcast.98), channel_id=1, source_target_pairs={{0,16},{4,20},{8,24},{12,28},{16,0},{20,4},{24,8},{28,12},{1,17},{... | collective-permute-start | bytes 3145736 | tf_op jit(solution)/shard_map/ppermute | solution.py:18
  168.5 8.7 %copy-start.5 = (f32[512,1024]{0,1:T(8,128)S(1)}, f32[512,1024]{0,1:T(8,128)}, u32[]{:S(2)}) copy-start(f32[512,1024]{0,1:T(8,128)} %copy.80) | copy-start | bytes 6291460
  168.5 8.7 %copy-start.6 = (f32[512,1024]{0,1:T(8,128)S(1)}, f32[512,1024]{0,1:T(8,128)}, u32[]{:S(2)}) copy-start(f32[512,1024]{0,1:T(8,128)} %copy.77) | copy-start | bytes 6291460
  177.2 2.2 copy-start.12
  182.4 115.3 %reduce-scatter.9.cloned.1.call-start = ((), (), s32[]{:S(2)}) async-start(), calls=%async_computation.7 | async-start | bytes 2359296
  233.6 6.7 %copy-start.10 = (f32[512,512]{0,1:T(8,128)S(1)}, f32[512,512]{0,1:T(8,128)}, u32[]{:S(2)}) copy-start(f32[512,512]{0,1:T(8,128)} %all-reduce.7.cloned.1.call-done) | copy-start | bytes 3145732
  257.0 118.5 %all-reduce.9.cloned.1.call-start = ((), (), s32[]{:S(2)}) async-start(), calls=%async_computation.4 | async-start | bytes 4194304 | tf_op jit(solution)/shard_map/psum | solution.py:31
  298.9 2.0 collective-permute-start.3
  303.1 18.5 %collective-permute-start.4 = (f32[2,64,1024]{2,1,0:T(8,128)}, f32[2,64,1024]{2,1,0:T(8,128)}, u32[]{:S(2)}, u32[]{:S(2)}) collective-permute-start(f32[2,64,1024]{2,1,0:T(8,128)} %copy.85), channel_id=1, source_target_pairs={{0,8},{4,12},{8,0},{12,4},{16,24},{20,28},{24,16},{28,20},{1,9},{5... | collective-permute-start | bytes 1572872 | tf_op jit(solution)/shard_map/ppermute | solution.py:18
  306.1 17.8 %copy-start.9 = (f32[1,2,64,1024]{2,3,1,0:T(8,128)S(1)}, f32[1,2,64,1024]{2,3,1,0:T(8,128)}, u32[]{:S(2)}) copy-start(f32[1,2,64,1024]{2,3,1,0:T(8,128)} %get-tuple-element.76) | copy-start | bytes 1572868
  306.2 163.7 %all-reduce.11.cloned.1.call-start = ((), (), s32[]{:S(2)}) async-start(), calls=%async_computation.5 | async-start | bytes 2097152 | tf_op jit(solution)/shard_map/psum | solution.py:31
  329.0 71.0 %collective-permute-start.5 = (f32[4,64,1024]{2,1,0:T(8,128)S(1)}, f32[4,64,1024]{2,1,0:T(8,128)}, u32[]{:S(2)}, u32[]{:S(2)}) collective-permute-start(f32[4,64,1024]{2,1,0:T(8,128)S(1)} %bitcast.100), channel_id=1, source_target_pairs={{0,16},{4,20},{8,24},{12,28},{16,0},{20,4},{24,8},{28,12},{1,17},{... | collective-permute-start | bytes 3145736 | tf_op jit(solution)/shard_map/ppermute | solution.py:18
  404.8 8.7 %copy-start.4 = (f32[512,1024]{0,1:T(8,128)S(1)}, f32[512,1024]{0,1:T(8,128)}, u32[]{:S(2)}) copy-start(f32[512,1024]{0,1:T(8,128)} %copy.92) | copy-start | bytes 6291460
  404.8 8.7 %copy-start.7 = (f32[512,1024]{0,1:T(8,128)S(1)}, f32[512,1024]{0,1:T(8,128)}, u32[]{:S(2)}) copy-start(f32[512,1024]{0,1:T(8,128)} %copy.89) | copy-start | bytes 6291460
  413.5 2.2 copy-start.13
  413.9 1.3 copy-start.3
  469.8 6.8 %copy-start.11 = (f32[512,512]{0,1:T(8,128)S(1)}, f32[512,512]{0,1:T(8,128)}, u32[]{:S(2)}) copy-start(f32[512,512]{0,1:T(8,128)} %all-reduce.11.cloned.1.call-done) | copy-start | bytes 3145732
  (3 other events, 3.9 us)
Sparse Core Ops, SparseCore 0:
  20.0 43.8 reduce-scatter.6
  68.5 71.0 all-reduce.4
  182.5 51.0 all-reduce.6
  257.1 40.5 reduce-scatter.8
  306.3 69.1 all-reduce.8
  418.8 51.0 all-reduce.10
